TPU v7x, 32 devices: a whole 2x2x4 slice. The times are simulated.
32 devices in a mesh: dp: 8 (over z, x), tensor: 4 (over y, core).
Axes of the slice: x: 2, y: 2, z: 4, core: 2. Of those that a mesh axis runs over, the one named last changes fastest.
Arguments:
- tokens: bfloat16 [8192, 1024], P('dp'), may hold values from -17 to 17
- views: int32 [1], replicated, may hold values from 2 to 8, as said below
- ln1_gain: float32 [1024], replicated, may hold values from 0.5 to 1.5
- ln1_bias: float32 [1024], replicated, may hold values from -3 to 3
- w_query: bfloat16 [1024, 1024], P(None, 'tensor'), may hold values from -0.25 to 0.25
- w_key: bfloat16 [1024, 1024], P(None, 'tensor'), may hold values from -0.25 to 0.25
- w_value: bfloat16 [1024, 1024], P(None, 'tensor'), may hold values from -0.1875 to 0.1875
- w_out: bfloat16 [1024, 1024], P('tensor'), may hold values from -1.5 to 1.5
- ln2_gain: float32 [1024], replicated, may hold values from 0.5 to 1.5
- ln2_bias: float32 [1024], replicated, may hold values from -3 to 3
- w_up: bfloat16 [1024, 4096], P(None, 'tensor'), may hold values from -0.1875 to 0.1875
- w_down: bfloat16 [4096, 1024], P('tensor'), may hold values from -0.09375 to 0.09375
- cotangent: bfloat16 [8192, 1024], P('dp'), may hold values from -6 to 6
Outputs:
- mixed: bfloat16 [8192, 1024], P('dp')
- tokens_grad: bfloat16 [8192, 1024], P('dp')
- ln1_gain_grad: float32 [1024], replicated
- ln1_bias_grad: float32 [1024], replicated
- w_query_grad: float32 [1024, 1024], P(None, 'tensor')
- w_key_grad: float32 [1024, 1024], P(None, 'tensor')
- w_value_grad: float32 [1024, 1024], P(None, 'tensor')
- w_out_grad: float32 [1024, 1024], P('tensor')
- ln2_gain_grad: float32 [1024], replicated
- ln2_bias_grad: float32 [1024], replicated
- w_up_grad: float32 [1024, 4096], P(None, 'tensor')
- w_down_grad: float32 [4096, 1024], P('tensor')
Inputs may be any that keep to these rules, and one draw needn't show every extreme that they name: Exactly one scene has 8 views.
All inputs are finite; a program needn't handle non-finite values.
Results may differ from a plain program's by a relative error of at most 0.025.
Values may be sent and summed in bfloat16 or wider, within the bound.
A program may use at most 192 MiB of HBM per device.

v0:
```python
from functools import partial
import math

import jax
import jax.numpy as jnp
from jax import lax
from jax.sharding import PartitionSpec as P

HEAD_DIM = 64
VIEW_TOK = 1024
MAX_VIEWS = 8


norm_eps = 1e-05


def swapped(block, axis, bit):
    count = lax.axis_size(axis)
    route = []
    for low in range(count):
        high = low | 1 << bit
        if high != low and high < count:
            route += [(low, high), (high, low)]
    return lax.ppermute(block, axis, route)


def layer_norm(values, gain, shift):
    row_mean = jnp.mean(values, axis=-1, keepdims=True)
    centered = values - row_mean
    inverse = lax.rsqrt(jnp.mean(centered * centered, axis=-1, keepdims=True) + norm_eps)
    normed = centered * inverse
    return (normed * gain + shift, normed, inverse)


def norm_back(grad_norm, normed, inverse, gain):
    scaled = grad_norm * gain
    grad_input = inverse * (
        scaled
        - jnp.mean(scaled, axis=-1, keepdims=True)
        - normed * jnp.mean(scaled * normed, axis=-1, keepdims=True)
    )
    return (grad_input, jnp.sum(grad_norm * normed, axis=0), jnp.sum(grad_norm, axis=0))


def join_pair(own_part, partner, position, bit_level):
    upper_half = position // 2**bit_level % 2 == 1
    return jnp.where(
        upper_half,
        jnp.concatenate([partner, own_part], axis=0),
        jnp.concatenate([own_part, partner], axis=0),
    )


def key_piece(key_values, first_row, block_rows, heads_local, head_dim, valid_count):
    inner_width = heads_local * head_dim
    portion = lax.dynamic_slice_in_dim(key_values, first_row, block_rows, 0)
    key_part = portion[:, :inner_width].reshape(block_rows, heads_local, head_dim)
    value_part = portion[:, inner_width:].reshape(block_rows, heads_local, head_dim)
    live_keys = first_row + jnp.arange(block_rows, dtype=jnp.int32) < valid_count
    return (key_part, value_part, live_keys)


def masked_scores(query_heads, key_part, live_keys, scale_factor):
    scores = (
        jnp.einsum("qhd,khd->hqk", query_heads, key_part, preferred_element_type=jnp.float32)
        * scale_factor
    )
    return jnp.where(live_keys[None, None, :], scores, -1000000000.0)


def attend(query_heads, key_values, valid_count, block_rows):
    row_count, heads_local, head_dim = query_heads.shape
    scale_factor = head_dim ** (-0.5)

    def attend_sweep_step(counter, running):
        run_max, norm_sum, accum = running
        first_row = counter * block_rows
        key_part, value_part, live_keys = key_piece(
            key_values, first_row, block_rows, heads_local, head_dim, valid_count
        )
        scores = masked_scores(query_heads, key_part, live_keys, scale_factor)
        new_max = jnp.maximum(run_max, jnp.max(scores, axis=-1))
        chance = jnp.where(live_keys[None, None, :], jnp.exp(scores - new_max[:, :, None]), 0.0)
        shrink = jnp.exp(run_max - new_max)
        norm_sum = norm_sum * shrink + jnp.sum(chance, axis=-1)
        accum = accum * shrink.T[:, :, None] + jnp.einsum(
            "hqk,khd->qhd",
            chance.astype(jnp.bfloat16),
            value_part,
            preferred_element_type=jnp.float32,
        )
        return (new_max, norm_sum, accum)

    initial = (
        jnp.full((heads_local, row_count), -1e30, jnp.float32),
        jnp.zeros((heads_local, row_count), jnp.float32),
        jnp.zeros((row_count, heads_local, head_dim), jnp.float32),
    )
    run_max, norm_sum, accum = lax.fori_loop(
        0, key_values.shape[0] // block_rows, attend_sweep_step, initial
    )
    return (accum / norm_sum.T[:, :, None], run_max + jnp.log(norm_sum))


def key_sweep(query_heads, grad_heads, log_norm, delta_rows, key_values, valid_count, block_rows):
    row_count, heads_local, head_dim = query_heads.shape
    inner_width = heads_local * head_dim
    scale_factor = head_dim ** (-0.5)
    total_rows = key_values.shape[0]

    def key_sweep_step(counter, running):
        first_row = counter * block_rows
        key_part, value_part, live_keys = key_piece(
            key_values, first_row, block_rows, heads_local, head_dim, valid_count
        )
        scores = masked_scores(query_heads, key_part, live_keys, scale_factor)
        chance = jnp.where(live_keys[None, None, :], jnp.exp(scores - log_norm[:, :, None]), 0.0)
        grad_chance = jnp.einsum(
            "qhd,khd->hqk", grad_heads, value_part, preferred_element_type=jnp.float32
        )
        grad_scores = (chance * (grad_chance - delta_rows[:, :, None])).astype(jnp.bfloat16)
        grad_query = (
            running[0]
            + jnp.einsum("hqk,khd->qhd", grad_scores, key_part, preferred_element_type=jnp.float32)
            * scale_factor
        )
        grad_key = (
            jnp.einsum("hqk,qhd->khd", grad_scores, query_heads, preferred_element_type=jnp.float32)
            * scale_factor
        )
        grad_value = jnp.einsum(
            "hqk,qhd->khd",
            chance.astype(jnp.bfloat16),
            grad_heads,
            preferred_element_type=jnp.float32,
        )
        grad_block = jnp.concatenate(
            [
                grad_key.reshape(block_rows, inner_width),
                grad_value.reshape(block_rows, inner_width),
            ],
            axis=1,
        )
        return (grad_query, lax.dynamic_update_slice_in_dim(running[1], grad_block, first_row, 0))

    initial = (
        jnp.zeros((row_count, heads_local, head_dim), jnp.float32),
        jnp.zeros((total_rows, 2 * inner_width), jnp.float32),
    )
    return lax.fori_loop(0, total_rows // block_rows, key_sweep_step, initial)


def shards(
    tokens,
    views,
    ln1_gain,
    ln1_bias,
    w_query,
    w_key,
    w_value,
    w_out,
    ln2_gain,
    ln2_bias,
    w_up,
    w_down,
    cotangent,
):
    row_count = tokens.shape[0]
    inner_width = w_query.shape[1]
    heads_local = inner_width // HEAD_DIM
    scene_slots = MAX_VIEWS * VIEW_TOK
    group_size = scene_slots // row_count
    bit_count = group_size.bit_length() - 1
    block_rows = math.gcd(scene_slots, 512)
    position = lax.axis_index("dp")
    scene_index = position // group_size
    block_index = position % group_size
    valid_count = lax.dynamic_index_in_dim(views, scene_index, keepdims=False) * VIEW_TOK
    row_live = block_index * row_count + jnp.arange(row_count, dtype=jnp.int32) < valid_count
    row_keep = row_live.astype(jnp.float32)[:, None]
    inputs = tokens.astype(jnp.float32)
    attn_norm, normed_first, inverse_first = layer_norm(inputs, ln1_gain, ln1_bias)
    attn_in = attn_norm.astype(jnp.bfloat16)
    query_low = jnp.dot(attn_in, w_query, preferred_element_type=jnp.float32).astype(jnp.bfloat16)
    key_low = jnp.dot(attn_in, w_key, preferred_element_type=jnp.float32).astype(jnp.bfloat16)
    value_low = jnp.dot(attn_in, w_value, preferred_element_type=jnp.float32).astype(jnp.bfloat16)
    query_heads = query_low.reshape(row_count, heads_local, HEAD_DIM)
    key_values = jnp.concatenate([key_low, value_low], axis=1)
    for bit_level in range(bit_count):
        partner = swapped(key_values, "dp", bit_level)
        key_values = join_pair(key_values, partner, position, bit_level)
    heads_out, log_norm = attend(query_heads, key_values, valid_count, block_rows)
    attn_heads = heads_out.reshape(row_count, inner_width).astype(jnp.bfloat16)
    attn_proj = lax.psum(
        jnp.dot(attn_heads, w_out, preferred_element_type=jnp.float32).astype(jnp.bfloat16),
        "tensor",
    ).astype(jnp.float32)
    resid = inputs + row_keep * attn_proj
    mlp_norm, normed_second, inverse_second = layer_norm(resid, ln2_gain, ln2_bias)
    mlp_in = mlp_norm.astype(jnp.bfloat16)
    up_proj = jnp.dot(mlp_in, w_up, preferred_element_type=jnp.float32)
    activated, gelu_pull = jax.vjp(partial(jax.nn.gelu, approximate=True), up_proj)
    act_low = activated.astype(jnp.bfloat16)
    mlp_proj = lax.psum(
        jnp.dot(act_low, w_down, preferred_element_type=jnp.float32).astype(jnp.bfloat16), "tensor"
    ).astype(jnp.float32)
    mixed = (resid + row_keep * mlp_proj).astype(jnp.bfloat16)
    grad_mixed = cotangent.astype(jnp.float32)
    grad_mlp = (row_keep * grad_mixed).astype(jnp.bfloat16)
    w_down_grad = jnp.dot(act_low.T, grad_mlp, preferred_element_type=jnp.float32)
    grad_act = jnp.dot(grad_mlp, w_down.T, preferred_element_type=jnp.float32)
    grad_up = gelu_pull(grad_act)[0].astype(jnp.bfloat16)
    w_up_grad = jnp.dot(mlp_in.T, grad_up, preferred_element_type=jnp.float32)
    grad_mlp_in = lax.psum(
        jnp.dot(grad_up, w_up.T, preferred_element_type=jnp.float32).astype(jnp.bfloat16), "tensor"
    ).astype(jnp.float32)
    grad_second, ln2_gain_grad, ln2_bias_grad = norm_back(
        grad_mlp_in, normed_second, inverse_second, ln2_gain
    )
    grad_resid = grad_mixed + grad_second
    grad_attn = (row_keep * grad_resid).astype(jnp.bfloat16)
    w_out_grad = jnp.dot(attn_heads.T, grad_attn, preferred_element_type=jnp.float32)
    grad_heads_low = jnp.dot(grad_attn, w_out.T, preferred_element_type=jnp.float32).astype(
        jnp.bfloat16
    )
    grad_heads = grad_heads_low.reshape(row_count, heads_local, HEAD_DIM)
    delta_rows = jnp.sum(grad_heads.astype(jnp.float32) * heads_out, axis=-1).T
    grad_query, grad_pairs = key_sweep(
        query_heads, grad_heads, log_norm, delta_rows, key_values, valid_count, block_rows
    )
    for bit_level in reversed(range(bit_count)):
        half_rows = grad_pairs.shape[0] // 2
        upper_half = position // 2**bit_level % 2 == 1
        kept_part = jnp.where(upper_half, grad_pairs[half_rows:], grad_pairs[:half_rows])
        given_part = jnp.where(upper_half, grad_pairs[:half_rows], grad_pairs[half_rows:])
        grad_pairs = kept_part + swapped(given_part.astype(jnp.bfloat16), "dp", bit_level).astype(
            given_part.dtype
        )
    grad_key_low = grad_pairs[:, :inner_width].astype(jnp.bfloat16)
    grad_value_low = grad_pairs[:, inner_width:].astype(jnp.bfloat16)
    grad_query_low = grad_query.reshape(row_count, inner_width).astype(jnp.bfloat16)
    grad_attn_in = lax.psum(
        (
            jnp.dot(grad_query_low, w_query.T, preferred_element_type=jnp.float32)
            + jnp.dot(grad_key_low, w_key.T, preferred_element_type=jnp.float32)
            + jnp.dot(grad_value_low, w_value.T, preferred_element_type=jnp.float32)
        ).astype(jnp.bfloat16),
        "tensor",
    ).astype(jnp.float32)
    grad_first, ln1_gain_grad, ln1_bias_grad = norm_back(
        grad_attn_in, normed_first, inverse_first, ln1_gain
    )
    tokens_grad = (grad_resid + grad_first).astype(jnp.bfloat16)
    w_query_grad = jnp.dot(attn_in.T, grad_query_low, preferred_element_type=jnp.float32)
    w_key_grad = jnp.dot(attn_in.T, grad_key_low, preferred_element_type=jnp.float32)
    w_value_grad = jnp.dot(attn_in.T, grad_value_low, preferred_element_type=jnp.float32)
    summed = (
        lax.psum(ln1_gain_grad.astype(jnp.bfloat16), "dp").astype(jnp.float32),
        lax.psum(ln1_bias_grad.astype(jnp.bfloat16), "dp").astype(jnp.float32),
        lax.psum(w_query_grad.astype(jnp.bfloat16), "dp").astype(jnp.float32),
        lax.psum(w_key_grad.astype(jnp.bfloat16), "dp").astype(jnp.float32),
        lax.psum(w_value_grad.astype(jnp.bfloat16), "dp").astype(jnp.float32),
        lax.psum(w_out_grad.astype(jnp.bfloat16), "dp").astype(jnp.float32),
        lax.psum(ln2_gain_grad.astype(jnp.bfloat16), "dp").astype(jnp.float32),
        lax.psum(ln2_bias_grad.astype(jnp.bfloat16), "dp").astype(jnp.float32),
        lax.psum(w_up_grad.astype(jnp.bfloat16), "dp").astype(jnp.float32),
        lax.psum(w_down_grad.astype(jnp.bfloat16), "dp").astype(jnp.float32),
    )
    return (
        mixed,
        tokens_grad,
        summed[0],
        summed[1],
        summed[2],
        summed[3],
        summed[4],
        summed[5],
        summed[6],
        summed[7],
        summed[8],
        summed[9],
    )


def solution(mesh):
    placed = (
        P("dp", None),
        P(),
        P(),
        P(),
        P(None, "tensor"),
        P(None, "tensor"),
        P(None, "tensor"),
        P("tensor", None),
        P(),
        P(),
        P(None, "tensor"),
        P("tensor", None),
        P("dp", None),
    )
    return jax.shard_map(
        shards,
        mesh=mesh,
        in_specs=placed,
        out_specs=(
            P("dp", None),
            P("dp", None),
            P(),
            P(),
            P(None, "tensor"),
            P(None, "tensor"),
            P(None, "tensor"),
            P("tensor", None),
            P(),
            P(),
            P(None, "tensor"),
            P("tensor", None),
        ),
        check_vma=False,
    )
```

profile of v0, /device:TPU:0, one launch (start us, length us, event | category | flops | bytes accessed | tf_op | source)
XLA Modules:
  0.0 1363.8 jit_solution(16652114717491773932)
XLA Ops:
  15.2 3.0 collective-permute-start
  18.2 23.5 %collective-permute-done = bf16[1024,512]{0,1:T(8,128)(2,1)} collective-permute-done((bf16[1024,512]{0,1:T(8,128)(2,1)}, bf16[1024,512]{0,1:T(8,128)(2,1)}, u32[]{:S(2)}, u32[]{:S(2)}) %collective-permute-start) | collective-permute-done | bytes 1048608 | tf_op jit(solution)/shard_map/ppermute | solution.py:24
  41.7 11.4 maximum_select_fusion.2
  54.8 45.3 %collective-permute-done.1 = bf16[2048,512]{0,1:T(8,128)(2,1)} collective-permute-done((bf16[2048,512]{0,1:T(8,128)(2,1)}, bf16[2048,512]{0,1:T(8,128)(2,1)}, u32[]{:S(2)}, u32[]{:S(2)}) %collective-permute-start.1) | collective-permute-done | bytes 2097184 | tf_op jit(solution)/shard_map/ppermute | solution.py:24
  100.1 6.5 maximum_select_fusion.1
  106.6 2.6 collective-permute-start.2
  112.2 176.4 %collective-permute-done.2 = bf16[4096,512]{0,1:T(8,128)(2,1)} collective-permute-done((bf16[4096,512]{0,1:T(8,128)(2,1)}, bf16[4096,512]{0,1:T(8,128)(2,1)}, u32[]{:S(2)}, u32[]{:S(2)}) %collective-permute-start.2) | collective-permute-done | bytes 4194336 | tf_op jit(solution)/shard_map/ppermute | solution.py:24
  288.6 10.9 maximum_select_fusion
  299.5 135.2 %while.34 = (s32[]{:T(128)}, f32[4,1024]{1,0:T(4,128)S(1)}, f32[4,1024]{1,0:T(4,128)S(1)}, f32[1024,4,64]{0,2,1:T(8,128)}, s32[]{:T(128)}, /*index=5*/bf16[8192,...) while((s32[]{:T(128)}, f32[4,1024]{1,0:T(4,128)S(1)}, ...), condition=%wide.region_5.6_spmd.clone, body=%wide.region_2.5_spmd.clone.sunk | while | flops 564945920 | bytes 38013192 | solution.py:99
  302.2 2.5 fusion.142
  439.0 52.3 %all-reduce.8.cloned.1.call-done = bf16[1024,1024]{1,0:T(8,128)(2,1)} async-done(((bf16[1024,1024]{1,0:T(8,128)(2,1)}), bf16[1024,1024]{1,0:T(8,128)(2,1)}) %all-reduce.8.cloned.1.call-update) | async-done | bytes 2097168 | tf_op jit(solution)/shard_map/psum | solution.py:194
  491.2 3.2 fusion.72
  495.9 2.6 fusion.71
  498.6 5.3 fusion.58
  505.2 3.7 convolution_convert_fusion.2
  509.0 51.5 %all-reduce.10.cloned.1.call-done = bf16[1024,1024]{1,0:T(8,128)(2,1)} async-done(((bf16[1024,1024]{1,0:T(8,128)(2,1)}), bf16[1024,1024]{1,0:T(8,128)(2,1)}) %all-reduce.10.cloned.1.call-update) | async-done | bytes 2097168 | tf_op jit(solution)/shard_map/psum | solution.py:214
  560.5 6.0 fusion.49
  572.7 7.8 broadcast_in_dim.119
  580.5 186.5 %while.35 = (s32[]{:T(128)}, f32[1024,4,64]{0,2,1:T(8,128)}, f32[8192,512]{0,1:T(8,128)}, bf16[8192,512]{0,1:T(8,128)(2,1)}, s32[]{:T(128)}, /*index=5*/bf16[102...) while((s32[]{:T(128)}, f32[1024,4,64]{0,2,1:T(8,128)}, ...), condition=%wide.region_15.16_spmd.clone, body=%wide.region_14.15_spmd.clone.sunk | while | flops 1368523776 | bytes 55363356 | solution.py:150
  585.1 3.4 multiply_convert_fusion.8
  596.7 3.4 multiply_convert_fusion.8
  608.4 3.4 multiply_convert_fusion.8
  620.1 3.4 multiply_convert_fusion.8
  631.7 3.4 multiply_convert_fusion.8
  643.4 3.4 multiply_convert_fusion.8
  655.0 3.4 multiply_convert_fusion.8
  666.7 3.4 multiply_convert_fusion.8
  678.3 3.4 multiply_convert_fusion.8
  690.0 3.4 multiply_convert_fusion.8
  701.6 3.4 multiply_convert_fusion.8
  713.3 3.4 multiply_convert_fusion.8
  725.0 3.4 multiply_convert_fusion.8
  736.6 3.4 multiply_convert_fusion.8
  748.3 3.4 multiply_convert_fusion.8
  759.9 3.4 multiply_convert_fusion.8
  767.0 6.2 select_convert_fusion
  775.7 180.4 %collective-permute-done.3 = bf16[4096,512]{0,1:T(8,128)(2,1)S(1)} collective-permute-done((bf16[4096,512]{0,1:T(8,128)(2,1)S(1)}, bf16[4096,512]{0,1:T(8,128)(2,1)S(1)}, u32[]{:S(2)}, u32[]{:S(2)}) %collective-permute-start.3) | collective-permute-done | bytes 4194336 | tf_op jit(solution)/shard_map/ppermute | solution.py:24
  956.2 7.2 convert_add_fusion
  964.4 46.1 %collective-permute-done.4 = bf16[2048,512]{0,1:T(8,128)(2,1)S(1)} collective-permute-done((bf16[2048,512]{0,1:T(8,128)(2,1)S(1)}, bf16[2048,512]{0,1:T(8,128)(2,1)S(1)}, u32[]{:S(2)}, u32[]{:S(2)}) %collective-permute-start.4) | collective-permute-done | bytes 2097184 | tf_op jit(solution)/shard_map/ppermute | solution.py:24
  1013.8 4.0 convolution_convert_fusion.3
  1018.7 17.0 %collective-permute-done.5 = bf16[1024,512]{0,1:T(8,128)(2,1)S(1)} collective-permute-done((bf16[1024,512]{0,1:T(8,128)(2,1)S(1)}, bf16[1024,512]{0,1:T(8,128)(2,1)S(1)}, u32[]{:S(2)}, u32[]{:S(2)}) %collective-permute-start.5) | collective-permute-done | bytes 1048608 | tf_op jit(solution)/shard_map/ppermute | solution.py:24
  1039.7 7.4 convolution_convert_fusion
  1047.1 4.2 convolution_convert_fusion.1
  1060.7 66.4 %all-reduce.14.cloned.1.call-done = (bf16[1024,1024]{1,0:T(8,128)(2,1)}, bf16[1024,1024]{1,0:T(8,128)(2,1)}) async-done(((bf16[1024,1024]{1,0:T(8,128)(2,1)}, bf16[1024,1024]{1,0:T(8,128)(2,1)}), (bf16[1024,1024]{1,0:T(8,128)(2,1)}, bf16[1024,1024]{1,0:T(8,128)(2,1)})) %all-reduce.14.cloned.1.call-update) | async-done | bytes 4194320 | tf_op jit(solution)/shard_map/psum | solution.py:204
  1129.1 3.5 fusion.51
  1132.6 23.0 %all-reduce = (bf16[1024]{0:T(1024)(128)(2,1)S(1)}, bf16[1024]{0:T(1024)(128)(2,1)S(1)}, bf16[1024]{0:T(1024)(128)(2,1)S(1)}, bf16[1024]{0:T(1024)(128)(2,1)S(1)}) all-reduce(bf16[1024]{0:T(1024)(128)(2,1)S(1)} %get-tuple-element.354, bf16[1024]{0:T(1024)(128)(2,1)S(1)} %reduce_sum.146, ...), channel_id=1, replica_groups=mesh['dp'=8,'tensor'=4] {'dp'}, use_global_device_ids=true, to_apply=%region_20.21 | all-reduce | flops 4096 | bytes 16384 | tf_op jit(solution)/shard_map/psum | solution.py:258
  1158.0 6.8 fusion.43
  1164.8 179.8 %all-reduce.12.cloned.1.call-done = (bf16[1024,256]{1,0:T(8,128)(2,1)}, bf16[1024,256]{1,0:T(8,128)(2,1)}, bf16[1024,256]{1,0:T(8,128)(2,1)}, bf16[256,1024]{1,0...) async-done(((bf16[1024,256]{1,0:T(8,128)(2,1)}, bf16[1024,256]{1,0:T(8,128)(2,1)}, bf16[1024,256]{1,0:T(8,128)(2,1)}, bf16[256,1024]{1,0:T(8,128)(2,1)}, ...) | async-done | bytes 6291472 | tf_op jit(solution)/shard_map/psum | solution.py:260
  (526 shorter events, 326.1 us)
Async XLA Ops:
  7.2 488.7 %copy-start = (bf16[1024,1024]{1,0:T(8,128)(2,1)S(1)}, bf16[1024,1024]{1,0:T(8,128)(2,1)}, u32[]{:S(2)}) copy-start(bf16[1024,1024]{1,0:T(8,128)(2,1)} %param.27) | copy-start | bytes 6291460
  7.2 4.5 copy-start.40
  7.2 4.5 copy-start.44
  7.2 5.4 copy-start.32
  7.2 484.0 %all-reduce.8.cloned.1.call-start = ((), (), s32[]{:S(2)}) async-start(), calls=%async_computation | async-start | bytes 4194304 | tf_op jit(solution)/shard_map/psum | solution.py:194
  7.3 4.5 copy-start.2
  9.4 4.0 copy-start.36
  15.2 26.4 %collective-permute-start = (bf16[1024,512]{0,1:T(8,128)(2,1)}, bf16[1024,512]{0,1:T(8,128)(2,1)}, u32[]{:S(2)}, u32[]{:S(2)}) collective-permute-start(bf16[1024,512]{0,1:T(8,128)(2,1)} %pad_maximum_fusion), channel_id=1, source_target_pairs={{0,4},{4,0},{8,12},{12,8},{16,20},{20,16},{24,28},{28,24},{1,5},{5... | collective-permute-start | bytes 3145736 | tf_op jit(solution)/shard_map/ppermute | solution.py:24
  53.0 47.1 %collective-permute-start.1 = (bf16[2048,512]{0,1:T(8,128)(2,1)}, bf16[2048,512]{0,1:T(8,128)(2,1)}, u32[]{:S(2)}, u32[]{:S(2)}) collective-permute-start(bf16[2048,512]{0,1:T(8,128)(2,1)} %maximum_select_fusion.2), channel_id=1, source_target_pairs={{0,8},{8,0},{4,12},{12,4},{16,24},{24,16},{20,28},{28,20},{1,9},{9... | collective-permute-start | bytes 6291464 | tf_op jit(solution)/shard_map/ppermute | solution.py:24
  54.8 55.0 %copy-start.28 = (bf16[1024,256]{1,0:T(8,128)(2,1)S(1)}, bf16[1024,256]{1,0:T(8,128)(2,1)}, u32[]{:S(2)}) copy-start(bf16[1024,256]{1,0:T(8,128)(2,1)} %param.21) | copy-start | bytes 1572868
  106.6 182.0 %collective-permute-start.2 = (bf16[4096,512]{0,1:T(8,128)(2,1)}, bf16[4096,512]{0,1:T(8,128)(2,1)}, u32[]{:S(2)}, u32[]{:S(2)}) collective-permute-start(bf16[4096,512]{0,1:T(8,128)(2,1)} %maximum_select_fusion.1), channel_id=1, source_target_pairs={{0,16},{16,0},{4,20},{20,4},{8,24},{24,8},{12,28},{28,12},{1,17},{... | collective-permute-start | bytes 12582920 | tf_op jit(solution)/shard_map/ppermute | solution.py:24
  299.5 137.3 %copy-start.27 = (bf16[256,1024]{1,0:T(8,128)(2,1)S(1)}, bf16[256,1024]{1,0:T(8,128)(2,1)}, u32[]{:S(2)}) copy-start(bf16[256,1024]{1,0:T(8,128)(2,1)} %param.24) | copy-start | bytes 1572868
  438.9 121.6 %all-reduce.10.cloned.1.call-start = ((), (), s32[]{:S(2)}) async-start(), calls=%async_computation.1 | async-start | bytes 4194304 | tf_op jit(solution)/shard_map/psum | solution.py:214
  438.9 57.0 %copy-start.42 = (f32[1024]{0:T(1024)S(1)}, f32[1024]{0:T(1024)}, u32[]{:S(2)}) copy-start(f32[1024]{0:T(1024)} %param.25) | copy-start | bytes 12292
  438.9 57.0 %copy-start.47 = (f32[1024]{0:T(1024)S(1)}, f32[1024]{0:T(1024)}, u32[]{:S(2)}) copy-start(f32[1024]{0:T(1024)} %param.26) | copy-start | bytes 12292
  491.2 3.2 copy-start.3
  491.2 3.5 copy-start.10
  498.6 5.3 copy-start.49
  508.9 57.6 %copy-start.4 = (bf16[1024,1024]{1,0:T(8,128)(2,1)S(1)}, bf16[1024,1024]{1,0:T(8,128)(2,1)}, u32[]{:S(2)}) copy-start(bf16[1024,1024]{1,0:T(8,128)(2,1)} %param.17) | copy-start | bytes 6291460
  508.9 618.2 %all-reduce.14.cloned.1.call-start = ((), (), s32[]{:S(2)}) async-start(), calls=%async_computation.3 | async-start | bytes 8388608 | tf_op jit(solution)/shard_map/psum | solution.py:204
  560.5 6.0 copy-start.11
  560.5 6.0 copy-start.13
  560.5 6.0 copy-start.26
  566.5 4.4 copy-start.18
  572.7 7.8 copy-start.35
  773.2 182.9 %collective-permute-start.3 = (bf16[4096,512]{0,1:T(8,128)(2,1)S(1)}, bf16[4096,512]{0,1:T(8,128)(2,1)S(1)}, u32[]{:S(2)}, u32[]{:S(2)}) collective-permute-start(bf16[4096,512]{0,1:T(8,128)(2,1)S(1)} %select_convert_fusion), channel_id=1, source_target_pairs={{0,16},{16,0},{4,20},{20,4},{8,24},{24,8},{12,28},{28,12},{1,17},{... | collective-permute-start | bytes 12582920 | tf_op jit(solution)/shard_map/ppermute | solution.py:24
  963.8 50.0 %copy-start.46 = (bf16[1024,1024]{1,0:T(8,128)(2,1)S(1)}, bf16[1024,1024]{1,0:T(8,128)(2,1)}, u32[]{:S(2)}) copy-start(bf16[1024,1024]{1,0:T(8,128)(2,1)} %param.28) | copy-start | bytes 6291460
  963.8 50.0 %copy-start.50 = (f32[1024,1024]{1,0:T(8,128)S(1)}, f32[1024,1024]{1,0:T(8,128)}, u32[]{:S(2)}) copy-start(f32[1024,1024]{1,0:T(8,128)} %copy-done.49) | copy-start | bytes 12582916
  963.8 46.7 %collective-permute-start.4 = (bf16[2048,512]{0,1:T(8,128)(2,1)S(1)}, bf16[2048,512]{0,1:T(8,128)(2,1)S(1)}, u32[]{:S(2)}, u32[]{:S(2)}) collective-permute-start(bf16[2048,512]{0,1:T(8,128)(2,1)S(1)} %select_convert_fusion.1), channel_id=1, source_target_pairs={{0,8},{8,0},{4,12},{12,4},{16,24},{24,16},{20,28},{28,20},{1,9},{9... | collective-permute-start | bytes 6291464 | tf_op jit(solution)/shard_map/ppermute | solution.py:24
  1012.2 5.6 copy-start.7
  1012.2 5.6 copy-start.29
  1012.3 23.4 %collective-permute-start.5 = (bf16[1024,512]{0,1:T(8,128)(2,1)S(1)}, bf16[1024,512]{0,1:T(8,128)(2,1)S(1)}, u32[]{:S(2)}, u32[]{:S(2)}) collective-permute-start(bf16[1024,512]{0,1:T(8,128)(2,1)S(1)} %select_convert_fusion.2), channel_id=1, source_target_pairs={{0,4},{4,0},{8,12},{12,8},{16,20},{20,16},{24,28},{28,24},{1,5},{5... | collective-permute-start | bytes 3145736 | tf_op jit(solution)/shard_map/ppermute | solution.py:24
  1017.9 18.4 %copy-start.21 = (bf16[1024,4,64]{0,2,1:T(8,128)(2,1)}, bf16[1024,4,64]{0,2,1:T(8,128)(2,1)S(1)}, u32[]{:S(2)}) copy-start(bf16[1024,4,64]{0,2,1:T(8,128)(2,1)S(1)} %convert_element_type.208) | copy-start | bytes 1572868
  1018.6 17.6 %copy-start.31 = (bf16[1024,256]{1,0:T(8,128)(2,1)S(1)}, bf16[1024,256]{1,0:T(8,128)(2,1)}, u32[]{:S(2)}) copy-start(bf16[1024,256]{1,0:T(8,128)(2,1)} %param.22) | copy-start | bytes 1572868
  1039.4 7.7 copy-start.48
  1039.4 305.1 %all-reduce.12.cloned.1.call-start = ((), (), s32[]{:S(2)}) async-start(), calls=%async_computation.2 | async-start | bytes 12582912 | tf_op jit(solution)/shard_map/psum | solution.py:260
  1039.7 7.4 copy-start.12
  1039.7 7.4 copy-start.52
  1047.1 4.2 copy-start.22
  1047.1 4.2 copy-start.24
  1058.6 70.5 %copy-start.37 = (f32[1024]{0:T(1024)S(1)}, f32[1024]{0:T(1024)}, u32[]{:S(2)}) copy-start(f32[1024]{0:T(1024)} %copy-done.36) | copy-start | bytes 12292
  1058.6 70.5 %copy-start.39 = (f32[1024]{0:T(1024)S(1)}, f32[1024]{0:T(1024)}, u32[]{:S(2)}) copy-start(f32[1024]{0:T(1024)} %copy-done.38) | copy-start | bytes 12292
  1058.6 70.5 %copy-start.41 = (f32[1024]{0:T(1024)S(1)}, f32[1024]{0:T(1024)}, u32[]{:S(2)}) copy-start(f32[1024]{0:T(1024)} %param.19) | copy-start | bytes 12292
  1058.7 73.9 %copy-start.43 = (bf16[1024]{0:T(1024)(128)(2,1)S(1)}, bf16[1024]{0:T(1024)(128)(2,1)}, u32[]{:S(2)}) copy-start(bf16[1024]{0:T(1024)(128)(2,1)} %get-tuple-element.352) | copy-start | bytes 6148
  1344.6 6.4 copy-start.34
  1344.6 7.5 copy-start.20
  1351.0 3.6 copy-start.19
  1352.1 5.0 copy-start.1
  (75 other events, 122.3 us)
Sparse Core Ops, SparseCore 0:
  439.0 52.2 all-reduce.7
  509.0 51.4 all-reduce.9
  1039.5 87.5 all-reduce.13
  1133.1 211.3 all-reduce.11
where the time goes:
time: 1370 us; the launch traced here: 1360 us
  waiting for transfers between devices  839 us (61%)
  matrix products  253 us (18%)
  other arithmetic  154 us (11%)
  local copies, waits for them, and re-layouts  65.7 us (5%)
  blocking collectives  23 us (2%)
  between operations  15.4 us (1%)
    ppermute x6, waiting for transfers between devices, swapped(): return lax.ppermute(block, axis, route)  489 us
    psum x1, waiting for transfers between devices, shards(): lax.psum(w_query_grad.astype(jnp.bfloat16), 'dp').astype(jnp.float32)  180 us
    psum x1, waiting for transfers between devices, shards(): lax.psum(jnp.dot(act_low, w_down, preferred_element_type=jnp.float32).ast...  66.4 us
    dot_general x16, matrix products, key_sweep_step(): jnp.einsum('qhd,khd->hqk', grad_heads, value_part, preferred_element_type...  54 us
    psum x1, waiting for transfers between devices, shards(): lax.psum(jnp.dot(attn_heads, w_out, preferred_element_type=jnp.float32).a...  52.3 us
    psum x1, waiting for transfers between devices, shards(): lax.psum(jnp.dot(grad_up, w_up.T, preferred_element_type=jnp.float32).ast...  51.5 us
    dot_general x32, matrix products, masked_scores(): jnp.einsum('qhd,khd->hqk', query_heads, key_part, preferred_element_type=...  46.3 us
    reduce_sum x16, other arithmetic, attend_sweep_step(): norm_sum = norm_sum * shrink + jnp.sum(chance, axis=-1)  40.7 us
  transfers between devices with their start and end apart: 10, of which 10 were waited for; matrix products, arithmetic and copies ran while one was open for 3% of the time, Pallas kernels for 0%

commit v1 on v0

v1 whole, which is shorter than its diff:
```python
from functools import partial
import math

import jax
import jax.numpy as jnp
from jax import lax
from jax.experimental import pallas as pl
from jax.experimental.pallas import tpu as pltpu
from jax.sharding import PartitionSpec as P

HEAD_DIM = 64
VIEW_TOK = 1024
MAX_VIEWS = 8
LOG2E = math.log2(math.e)
VMEM_BYTES = 56 << 20

norm_eps = 1e-05
bf16 = jnp.bfloat16
f32 = jnp.float32
dot = partial(jnp.dot, preferred_element_type=f32)


def contract(left, right, left_dim, right_dim):
    return lax.dot_general(
        left, right, (((left_dim,), (right_dim,)), ((), ())), preferred_element_type=f32
    )


def layer_norm(values, gain, shift):
    row_mean = jnp.mean(values, axis=-1, keepdims=True)
    centered = values - row_mean
    inverse = lax.rsqrt(jnp.mean(centered * centered, axis=-1, keepdims=True) + norm_eps)
    normed = centered * inverse
    return (normed * gain + shift, normed, inverse)


def norm_back(grad_norm, normed, inverse, gain):
    scaled = grad_norm * gain
    grad_input = inverse * (
        scaled
        - jnp.mean(scaled, axis=-1, keepdims=True)
        - normed * jnp.mean(scaled * normed, axis=-1, keepdims=True)
    )
    return (grad_input, jnp.sum(grad_norm * normed, axis=0), jnp.sum(grad_norm, axis=0))


def sweep_forward(live_views, q_pad, kv, v_ones, carry, last):
    count = q_pad.shape[1]
    keys = kv.shape[0]
    sum_rows = v_ones.shape[0]
    bq, bk = 2048, 512

    def kernel(*refs):
        live_ref, q_ref, kv_ref, v_ref = refs[:4]
        refs = refs[4:]
        if carry is not None:
            start = (refs[0][...], refs[1][...])
            refs = refs[2:]
        else:
            start = (jnp.full((1, bq), -1e30, f32), jnp.zeros((sum_rows, bq), f32))
        queries = q_ref[...]

        def view_step(view, running):
            top, accum = running
            for part in range(VIEW_TOK // bk):
                first = pl.multiple_of(view * VIEW_TOK + part * bk, bk)
                scores = dot(kv_ref[pl.ds(first, bk), :], queries)
                new_top = jnp.maximum(top, jnp.max(scores, axis=0, keepdims=True))
                weights = jnp.exp2(scores - new_top).astype(bf16)
                accum = accum * jnp.exp2(top - new_top) + dot(v_ref[:, pl.ds(first, bk)], weights)
                top = new_top
            return (top, accum)

        top, accum = lax.fori_loop(0, live_ref[0], view_step, start)
        if last:
            total = accum[HEAD_DIM : HEAD_DIM + 1]
            heads_out = accum[:HEAD_DIM] / total
            refs[0][...] = heads_out
            refs[1][...] = heads_out.astype(bf16)
            refs[2][...] = top + jnp.log2(total)
        else:
            refs[0][...] = top
            refs[1][...] = accum

    def columns(rows):
        return pl.BlockSpec((rows, bq), lambda i: (0, i))

    whole = [
        pl.BlockSpec((keys, kv.shape[1]), lambda i: (0, 0)),
        pl.BlockSpec((sum_rows, keys), lambda i: (0, 0)),
    ]
    in_specs = [pl.BlockSpec(memory_space=pltpu.SMEM), columns(q_pad.shape[0])] + whole
    operands = [live_views, q_pad, kv, v_ones]
    if carry is not None:
        in_specs += [columns(1), columns(sum_rows)]
        operands += list(carry)
    if last:
        shapes = [((HEAD_DIM, count), f32), ((HEAD_DIM, count), bf16), ((1, count), f32)]
    else:
        shapes = [((1, count), f32), ((sum_rows, count), f32)]
    return pl.pallas_call(
        kernel,
        grid=(count // bq,),
        in_specs=in_specs,
        out_specs=[columns(shape[0]) for shape, _ in shapes],
        out_shape=[jax.ShapeDtypeStruct(shape, kind) for shape, kind in shapes],
        compiler_params=pltpu.CompilerParams(vmem_limit_bytes=VMEM_BYTES),
        cost_estimate=pl.CostEstimate(
            flops=16 * HEAD_DIM * count * keys, bytes_accessed=8 << 20, transcendentals=count * keys
        ),
    )(*operands)


def sweep_backward(live_views, q_pad, g_pad, q_rows, g_rows, kv, k_cols, log_norm, delta, carry):
    count = q_pad.shape[1]
    keys = kv.shape[0]
    bq, bk = 1024, 512
    last = carry is not None

    def kernel(*refs):
        live_ref, q_ref, g_ref, qr_ref, gr_ref, kv_ref, kc_ref, norm_ref, delta_ref = refs[:9]
        carry_ref = refs[9] if last else None
        pairs_ref, out_ref, total_ref = refs[-3:]
        step = pl.program_id(0)

        @pl.when(step == 0)
        def _():
            total_ref[...] = carry_ref[...] if last else jnp.zeros_like(total_ref)

        live = step * bk < live_ref[0] * VIEW_TOK

        @pl.when(live)
        def _():
            key_values = kv_ref[...]
            key_columns = kc_ref[...]
            accum = jnp.zeros((bk, 2 * HEAD_DIM), f32)
            for part in range(count // bq):
                span = pl.ds(part * bq, bq)
                scores = dot(key_values, q_ref[:, span])
                weights = jnp.exp2(scores - norm_ref[:, span])
                grad_weights = dot(key_values, g_ref[:, span])
                grad_scores = (weights * (grad_weights - delta_ref[:, span])).astype(bf16)
                accum += dot(weights.astype(bf16), gr_ref[span, :])
                accum += dot(grad_scores, qr_ref[span, :])
                total_ref[:, span] += dot(key_columns, grad_scores)
            lane = lax.broadcasted_iota(jnp.int32, accum.shape, 1)
            pairs_ref[...] = jnp.where(lane < HEAD_DIM, accum * (1.0 / LOG2E), accum).astype(bf16)

        @pl.when(jnp.logical_not(live))
        def _():
            pairs_ref[...] = jnp.zeros_like(pairs_ref)

        @pl.when(step == pl.num_programs(0) - 1)
        def _():
            if last:
                out_ref[...] = (total_ref[...] * HEAD_DIM ** (-0.5)).astype(bf16)
            else:
                out_ref[...] = total_ref[...]

    def whole(array):
        return pl.BlockSpec(array.shape, lambda i: (0, 0))

    in_specs = [
        pl.BlockSpec(memory_space=pltpu.SMEM),
        whole(q_pad),
        whole(g_pad),
        whole(q_rows),
        whole(g_rows),
        pl.BlockSpec((bk, 2 * HEAD_DIM), lambda i: (i, 0)),
        pl.BlockSpec((HEAD_DIM, bk), lambda i: (0, i)),
        whole(log_norm),
        whole(delta),
    ]
    operands = [live_views, q_pad, g_pad, q_rows, g_rows, kv, k_cols, log_norm, delta]
    if last:
        in_specs.append(whole(carry))
        operands.append(carry)
    return pl.pallas_call(
        kernel,
        grid=(keys // bk,),
        in_specs=in_specs,
        out_specs=[
            pl.BlockSpec((bk, 2 * HEAD_DIM), lambda i: (i, 0)),
            pl.BlockSpec((HEAD_DIM, count), lambda i: (0, 0)),
        ],
        out_shape=[
            jax.ShapeDtypeStruct((keys, 2 * HEAD_DIM), bf16),
            jax.ShapeDtypeStruct((HEAD_DIM, count), bf16 if last else f32),
        ],
        scratch_shapes=[pltpu.VMEM((HEAD_DIM, count), f32)],
        compiler_params=pltpu.CompilerParams(vmem_limit_bytes=VMEM_BYTES),
        cost_estimate=pl.CostEstimate(
            flops=40 * HEAD_DIM * count * keys, bytes_accessed=10 << 20, transcendentals=count * keys
        ),
    )(*operands)


def shards(
    tokens,
    views,
    ln1_gain,
    ln1_bias,
    w_query,
    w_key,
    w_value,
    w_out,
    ln2_gain,
    ln2_bias,
    w_up,
    w_down,
    cotangent,
):
    row_count, width = tokens.shape
    inner = w_query.shape[1]
    heads = inner // HEAD_DIM
    half = row_count // 2
    group = MAX_VIEWS * VIEW_TOK // row_count
    devices = lax.axis_size("dp")
    assert row_count == VIEW_TOK and group == 2 * heads and lax.axis_size("tensor") == 4
    position = lax.axis_index("dp")
    block = position % group
    side = block % 2
    core = lax.axis_index("tensor") % 2
    scene_views = lax.dynamic_index_in_dim(views, position // group, keepdims=False)
    own_views = ((scene_views + 1 - side) // 2).reshape(1)
    far_views = ((scene_views + side) // 2).reshape(1)
    keep = (block < scene_views).astype(f32)
    lanes = [
        [first + 2 * place + bit for place in range(heads)]
        for first in range(0, devices, group)
        for bit in range(2)
    ]

    def exchange(block, split, concat):
        return lax.all_to_all(
            block, "dp", split, concat, axis_index_groups=lanes, tiled=True
        )

    def across(block):
        return lax.ppermute(block, "dp", [(i, i ^ 1) for i in range(devices)])

    def other_core(block):
        return lax.ppermute(block, "tensor", [(i, i ^ 1) for i in range(4)])

    def other_chip(block):
        return lax.ppermute(block, "tensor", [(i, i ^ 2) for i in range(4)])

    def own_first(block):
        return jnp.where(core == 0, block, jnp.concatenate([block[half:], block[:half]], axis=0))

    def own_rows_sum(far_part, own_part):
        arrived = other_core(far_part().astype(bf16))
        pair = (own_part() + arrived.astype(f32)).astype(bf16)
        return pair.astype(f32) + other_chip(pair).astype(f32)

    def both_halves(own):
        return jnp.concatenate([own, other_core(own)], axis=0)

    rows = own_first(tokens)
    grad_rows = own_first(cotangent)
    inputs_own = rows[:half].astype(f32)
    grad_own = grad_rows[:half].astype(f32)

    attn_norm, normed_first, inverse_first = layer_norm(rows.astype(f32), ln1_gain, ln1_bias)
    attn_in = attn_norm.astype(bf16)
    w_pairs = jnp.concatenate(
        [w_key.reshape(width, heads, HEAD_DIM), w_value.reshape(width, heads, HEAD_DIM)], axis=2
    ).reshape(width, 2 * inner)
    kv_low = dot(attn_in, w_pairs).astype(bf16)
    kv_own = exchange(kv_low, 1, 0)
    query_low = (contract(w_query, attn_in, 0, 1) * (LOG2E * HEAD_DIM ** (-0.5))).astype(bf16)
    q_cols = exchange(query_low, 0, 1)
    kv_far = across(kv_own)

    empty = jnp.zeros_like(q_cols)
    q_pad = jnp.concatenate([q_cols, empty], axis=0)

    def value_columns(kv):
        cols = kv.T
        ones = jnp.ones((16, cols.shape[1]), bf16)
        return cols[:HEAD_DIM], jnp.concatenate([cols[HEAD_DIM:], ones], axis=0)

    k_own, v_own = value_columns(kv_own)
    carry = sweep_forward(own_views, q_pad, kv_own, v_own, None, False)
    k_far, v_far = value_columns(kv_far)
    heads_out, heads_low, log_norm = sweep_forward(far_views, q_pad, kv_far, v_far, carry, True)
    attn_cols = exchange(heads_low, 1, 0)

    resid = inputs_own + keep * own_rows_sum(
        lambda: contract(attn_cols[:, half:], w_out, 0, 0),
        lambda: contract(attn_cols[:, :half], w_out, 0, 0),
    )
    mlp_norm, normed_second, inverse_second = layer_norm(resid, ln2_gain, ln2_bias)
    mlp_in = both_halves(mlp_norm.astype(bf16))
    up_proj = dot(mlp_in, w_up)
    activated, gelu_pull = jax.vjp(partial(jax.nn.gelu, approximate=True), up_proj)
    act_low = activated.astype(bf16)
    grad_mlp = (keep * grad_rows.astype(f32)).astype(bf16)
    grad_act = contract(grad_mlp, w_down, 1, 1)
    grad_up = gelu_pull(grad_act)[0].astype(bf16)
    grad_mlp_in = own_rows_sum(
        lambda: contract(grad_up[half:], w_up, 1, 1), lambda: contract(grad_up[:half], w_up, 1, 1)
    )
    mlp_proj = own_rows_sum(
        lambda: dot(act_low[half:], w_down), lambda: dot(act_low[:half], w_down)
    )
    mixed_own = (resid + keep * mlp_proj).astype(bf16)
    grad_second, ln2_gain_grad, ln2_bias_grad = norm_back(
        grad_mlp_in, normed_second, inverse_second, ln2_gain
    )
    grad_resid = grad_own + grad_second
    grad_attn = both_halves((keep * grad_resid).astype(bf16))
    grad_heads = contract(w_out, grad_attn, 1, 1).astype(bf16)
    g_cols = exchange(grad_heads, 0, 1)

    w_down_grad = contract(act_low, grad_mlp, 0, 0)
    w_up_grad = contract(mlp_in, grad_up, 0, 0)
    w_out_grad = dot(attn_cols, grad_attn)
    early = lax.psum((w_up_grad.astype(bf16), w_down_grad.astype(bf16), w_out_grad.astype(bf16)), "dp")

    g_pad = jnp.concatenate([empty, g_cols], axis=0)
    delta = jnp.sum(g_cols.astype(f32) * heads_out, axis=0, keepdims=True)
    q_rows = q_pad.T
    g_rows = g_pad.T
    pairs_far, carry = sweep_backward(
        far_views, q_pad, g_pad, q_rows, g_rows, kv_far, k_far, log_norm, delta, None
    )
    arrived = across(pairs_far)
    pairs_own, dq_cols = sweep_backward(
        own_views, q_pad, g_pad, q_rows, g_rows, kv_own, k_own, log_norm, delta, carry
    )
    pairs = (pairs_own.astype(f32) + arrived.astype(f32)).astype(bf16)
    grad_pairs = exchange(
        pairs.reshape(heads, row_count, 2 * HEAD_DIM), 0, 2
    ).reshape(row_count, 2 * inner)
    grad_query = exchange(dq_cols, 1, 0)

    def partial_in(start):
        return contract(grad_query[:, start : start + half], w_query, 0, 1) + contract(
            grad_pairs[start : start + half], w_pairs, 1, 1
        )

    grad_attn_in = own_rows_sum(lambda: partial_in(half), lambda: partial_in(0))
    grad_first, ln1_gain_grad, ln1_bias_grad = norm_back(
        grad_attn_in, normed_first[:half], inverse_first[:half], ln1_gain
    )
    tokens_grad_own = (grad_resid + grad_first).astype(bf16)

    w_query_grad = contract(attn_in, grad_query, 0, 1)
    w_pairs_grad = contract(attn_in, grad_pairs, 0, 0)
    late, early = lax.optimization_barrier(
        ((w_query_grad.astype(bf16), w_pairs_grad.astype(bf16)), early)
    )
    late = lax.psum(late, "dp")
    w_pairs_grad = late[1].astype(f32).reshape(width, heads, 2 * HEAD_DIM)
    small = jnp.stack([ln1_gain_grad, ln1_bias_grad, ln2_gain_grad, ln2_bias_grad]) * 0.5
    small = lax.psum(small, ("dp", "tensor"))

    def in_order(own):
        far = other_core(own)
        return jnp.where(
            core == 0, jnp.concatenate([own, far], axis=0), jnp.concatenate([far, own], axis=0)
        )

    return (
        in_order(mixed_own),
        in_order(tokens_grad_own),
        small[0],
        small[1],
        late[0].astype(f32),
        w_pairs_grad[:, :, :HEAD_DIM].reshape(width, inner),
        w_pairs_grad[:, :, HEAD_DIM:].reshape(width, inner),
        early[2].astype(f32),
        small[2],
        small[3],
        early[0].astype(f32),
        early[1].astype(f32),
    )


def solution(mesh):
    placed = (
        P("dp", None),
        P(),
        P(),
        P(),
        P(None, "tensor"),
        P(None, "tensor"),
        P(None, "tensor"),
        P("tensor", None),
        P(),
        P(),
        P(None, "tensor"),
        P("tensor", None),
        P("dp", None),
    )
    return jax.shard_map(
        shards,
        mesh=mesh,
        in_specs=placed,
        out_specs=(
            P("dp", None),
            P("dp", None),
            P(),
            P(),
            P(None, "tensor"),
            P(None, "tensor"),
            P(None, "tensor"),
            P("tensor", None),
            P(),
            P(),
            P(None, "tensor"),
            P("tensor", None),
        ),
        check_vma=False,
    )
```

time: 1370 us -> 591 us (0.43)
  waiting for transfers between devices: 839 us -> 207 us
  matrix products: 253 us -> 42 us
  Pallas kernels: 0 us -> 151 us
  other arithmetic: 154 us -> 41 us
  blocking collectives: 23 us -> 54.1 us
  local copies, waits for them, and re-layouts: 65.7 us -> 45.5 us
  starting transfers between devices: 12.3 us -> 29.7 us
    ppermute x6 -> x14, waiting for transfers between devices: 489 us -> 91 us  [the longest x4 84.8 us: other_chip(): return lax.ppermute(block, 'tensor', [(i, i ^ 2) for i in range(4)])]
    psum x4 -> x2, waiting for transfers between devices: 350 us -> 17.2 us  [the longest x1 17.2 us: shards(): late = lax.psum(late, 'dp')]
    dot_general x130 -> x20, matrix products: 253 us -> 42 us  [the longest x15 31.2 us: contract(): lax.dot_general(left, right, (((left_dim,), (right_dim,)), ((), ())), pre...]
    pallas_call x0 -> x4, Pallas kernels: none -> 151 us  [the longest x2 99.7 us: sweep_backward(): pl.pallas_call(kernel, grid=(keys // bk,), in_specs=in_specs, out_specs=[...]
    all_to_all x0 -> x5, waiting for transfers between devices: none -> 98.6 us  [exchange(): lax.all_to_all(block, 'dp', split, concat, axis_index_groups=lanes, tiled...]
    reduce_sum x18 -> x1, other arithmetic: 44.7 us -> 3.08 us  [shards(): delta = jnp.sum(g_cols.astype(f32) * heads_out, axis=0, keepdims=True)]
    slice x32 -> x9, local copies, waits for them, and re-layouts: 34.2 us -> 5.98 us  [the longest x2 3 us: value_columns(): return (cols[:HEAD_DIM], jnp.concatenate([cols[HEAD_DIM:], ones], axis=0))]
    all_to_all x0 -> x5, starting transfers between devices: none -> 21.4 us  [exchange(): lax.all_to_all(block, 'dp', split, concat, axis_index_groups=lanes, tiled...]
  transfers between devices with their start and end apart: 10 -> 21, of which waited for: 10 -> 14; matrix products, arithmetic and copies ran while one was open for 3% -> 13% of each run, Pallas kernels for 0% -> 21%
where the time goes in v1:
time: 591 us; the launch traced here: 586 us
  waiting for transfers between devices  207 us (35%)
  Pallas kernels  151 us (26%)
  blocking collectives  54.1 us (9%)
  local copies, waits for them, and re-layouts  45.5 us (8%)
  matrix products  42 us (7%)
  other arithmetic  41 us (7%)
  starting transfers between devices  29.7 us (5%)
  between operations  15.6 us (3%)
    pallas_call x2, Pallas kernels, sweep_backward(): pl.pallas_call(kernel, grid=(keys // bk,), in_specs=in_specs, out_specs=[...  99.7 us
    all_to_all x5, waiting for transfers between devices, exchange(): lax.all_to_all(block, 'dp', split, concat, axis_index_groups=lanes, tiled...  98.6 us
    ppermute x4, waiting for transfers between devices, other_chip(): return lax.ppermute(block, 'tensor', [(i, i ^ 2) for i in range(4)])  84.8 us
    pallas_call x2, Pallas kernels, sweep_forward(): pl.pallas_call(kernel, grid=(count // bq,), in_specs=in_specs, out_specs=...  51.4 us
    psum x1, blocking collectives, shards(): small = lax.psum(small, ('dp', 'tensor'))  37.4 us
    dot_general x15, matrix products, contract(): lax.dot_general(left, right, (((left_dim,), (right_dim,)), ((), ())), pre...  31.2 us
    all_to_all x5, starting transfers between devices, exchange(): lax.all_to_all(block, 'dp', split, concat, axis_index_groups=lanes, tiled...  21.4 us
    psum x1, waiting for transfers between devices, shards(): late = lax.psum(late, 'dp')  17.2 us
  transfers between devices with their start and end apart: 21, of which 14 were waited for; matrix products, arithmetic and copies ran while one was open for 13% of the time, Pallas kernels for 21%

profile of v1, /device:TPU:0, one launch (start us, length us, event | category | flops | bytes accessed | tf_op | source)
XLA Modules:
  0.0 586.0 jit_solution(7150430022664241722)
XLA Ops:
  11.1 2.9 fusion
  16.8 6.3 %all-to-all-start = ((bf16[4,64,1024]{2,1,0:T(8,128)(2,1)}), bf16[4,64,1024]{2,1,0:T(8,128)(2,1)S(1)}, u32[]{:S(2)}, u32[]{:S(2)}) async-start(bf16[4,64,1024]{2,1,0:T(8,128)(2,1)} %bitcast.3), calls=%async_computation | async-start | bytes 1048576 | tf_op jit(solution)/shard_map/all_to_all | solution.py:235
  28.7 2.3 convolution_convert_fusion.6
  31.0 6.7 %all-to-all-done = bf16[4,64,1024]{2,1,0:T(8,128)(2,1)S(1)} async-done(((bf16[4,64,1024]{2,1,0:T(8,128)(2,1)}), bf16[4,64,1024]{2,1,0:T(8,128)(2,1)S(1)}, u32[]{:S(2)}, u32[]{:S(2)}) %all-to-all-start) | async-done | bytes 524320 | tf_op jit(solution)/shard_map/all_to_all | solution.py:235
  37.7 4.5 all-to-all-start.1
  45.6 2.1 concatenate.40.clone.refs_1_
  47.7 19.9 %all-to-all-done.1 = bf16[1024,4,128]{0,2,1:T(8,128)(2,1)} async-done(((bf16[1024,4,128]{0,2,1:T(8,128)(2,1)}), bf16[1024,4,128]{0,2,1:T(8,128)(2,1)}, u32[]{:S(2)}, u32[]{:S(2)}) %all-to-all-start.1) | async-done | bytes 1048608 | tf_op jit(solution)/shard_map/all_to_all | solution.py:235
  67.6 2.3 copy.86
  69.8 2.3 copy.66.refs_2_.refs_5_
  73.6 2.1 fusion.52
  76.6 23.8 %shard_map.220 = (f32[1,4096]{1,0:T(1,128)}, f32[80,4096]{1,0:T(8,128)}) custom-call(s32[1]{0:T(128)} %bitcast.12.refs_0_, bf16[128,4096]{1,0:T(8,128)(2,1)} %concatenate.40.clone.refs_1_, bf16[4096,128]{1,0:T(8,128)(2,1)} %copy.66.refs_2_.refs_5_, bf16[80,4096]{1,0:T(8,128)(2,1)} %concatenate.43.refs_3_), custom_call_target="tpu_custom_call" | custom-call | flops 17179869184 | bytes 8388608 | tf_op jit(solution)/shard_map/pallas_call | solution.py:101
  103.1 2.3 copy.68.refs_2_.refs_5_
  105.4 27.7 %shard_map.221 = (f32[64,4096]{1,0:T(8,128)}, bf16[64,4096]{1,0:T(8,128)(2,1)}, f32[1,4096]{1,0:T(1,128)}) custom-call(s32[1]{0:T(128)} %bitcast.1.refs_0_, bf16[128,4096]{1,0:T(8,128)(2,1)} %concatenate.40.clone.refs_1_, bf16[4096,128]{1,0:T(8,128)(2,1)} %copy.68.refs_2_.refs_5_, bf16[80,4096]{1,0:T(8,128)(2,1)} %concatenate.42.refs_3_, ...), custom_call_target="tpu_custom_call" | custom-call | flops 17179869184 | bytes 8388608 | tf_op jit(solution)/shard_map/pallas_call | solution.py:101
  134.2 16.7 %all_to_all.110 = bf16[64,4,1024]{2,0,1:T(8,128)(2,1)S(1)} all-to-all(bf16[64,4,1024]{2,0,1:T(8,128)(2,1)S(1)} %bitcast.111), channel_id=1, replica_groups={{0,8,16,24},{4,12,20,28},{1,9,17,25},{5,13,21,29},{2,10,18,26},{6,14,22..., dimensions={1} | all-to-all | bytes 1048576 | tf_op jit(solution)/shard_map/all_to_all | solution.py:235
  151.5 2.6 collective-permute-done.1
  157.1 24.0 %collective-permute-done.2 = bf16[512,1024]{1,0:T(8,128)(2,1)} collective-permute-done((bf16[512,1024]{1,0:T(8,128)(2,1)}, bf16[512,1024]{1,0:T(8,128)(2,1)}, u32[]{:S(2)}, u32[]{:S(2)}) %collective-permute-start.2) | collective-permute-done | bytes 1048608 | tf_op jit(solution)/shard_map/ppermute | solution.py:246
  181.1 2.4 fusion.46
  187.3 3.0 multiply_convert_fusion.1
  190.4 5.0 fusion.9
  204.1 22.7 %collective-permute-done.8 = bf16[512,1024]{1,0:T(8,128)(2,1)S(1)} collective-permute-done((bf16[512,1024]{1,0:T(8,128)(2,1)S(1)}, bf16[512,1024]{1,0:T(8,128)(2,1)S(1)}, u32[]{:S(2)}, u32[]{:S(2)}) %collective-permute-start.8) | collective-permute-done | bytes 1048608 | tf_op jit(solution)/shard_map/ppermute | solution.py:246
  227.9 20.5 %collective-permute-done.5 = bf16[512,1024]{1,0:T(8,128)(2,1)S(1)} collective-permute-done((bf16[512,1024]{1,0:T(8,128)(2,1)S(1)}, bf16[512,1024]{1,0:T(8,128)(2,1)S(1)}, u32[]{:S(2)}, u32[]{:S(2)}) %collective-permute-start.5) | collective-permute-done | bytes 1048608 | tf_op jit(solution)/shard_map/ppermute | solution.py:246
  248.5 2.9 multiply_convert_fusion.2
  254.8 3.2 fusion.20
  258.0 3.5 all-to-all-start.3
  261.8 5.5 convolution_convert_fusion
  267.3 3.8 convolution_convert_fusion.1
  271.1 3.0 fusion.21
  274.2 2.4 all-to-all-done.3
  278.9 3.1 multiply_reduce_fusion.3
  283.0 49.9 %shard_map.222 = (bf16[4096,128]{1,0:T(8,128)(2,1)}, f32[64,4096]{1,0:T(8,128)}) custom-call(s32[1]{0:T(128)} %bitcast.1.refs_0_, bf16[128,4096]{1,0:T(8,128)(2,1)} %concatenate.40.clone.refs_1_, bf16[128,4096]{1,0:T(8,128)(2,1)} %concatenate.49.clone.refs_2_, bf16[4096,128]{1,0:T(8,128)(2,1)} %pad_bitcast_fusion.1.refs_3_, ...), custom_call_target="tpu_custom_call" | custom-call | flops 42949672960 | bytes 10485760 | tf_op jit(solution)/shard_map/pallas_call | solution.py:178
  333.2 49.8 %shard_map.223 = (bf16[4096,128]{1,0:T(8,128)(2,1)}, bf16[64,4096]{1,0:T(8,128)(2,1)}) custom-call(s32[1]{0:T(128)} %bitcast.12.refs_0_, bf16[128,4096]{1,0:T(8,128)(2,1)} %concatenate.40.clone.refs_1_, bf16[128,4096]{1,0:T(8,128)(2,1)} %concatenate.49.clone.refs_2_, bf16[4096,128]{1,0:T(8,128)(2,1)} %pad_bitcast_fusion.1.refs_3_, ...), custom_call_target="tpu_custom_call" | custom-call | flops 42949672960 | bytes 10485760 | tf_op jit(solution)/shard_map/pallas_call | solution.py:178
  384.9 3.5 all-to-all-start.4
  391.2 18.9 %all-to-all-done.4 = bf16[64,4,1024]{2,0,1:T(8,128)(2,1)S(1)} async-done(((bf16[64,4,1024]{2,0,1:T(8,128)(2,1)}), bf16[64,4,1024]{2,0,1:T(8,128)(2,1)S(1)}, u32[]{:S(2)}, u32[]{:S(2)}) %all-to-all-start.4) | async-done | bytes 524320 | tf_op jit(solution)/shard_map/all_to_all | solution.py:235
  410.1 3.5 all-to-all-start.5
  415.6 50.7 %all-to-all-done.5 = bf16[4,1024,128]{1,2,0:T(8,128)(2,1)S(1)} async-done(((bf16[4,1024,128]{1,2,0:T(8,128)(2,1)}), bf16[4,1024,128]{1,2,0:T(8,128)(2,1)S(1)}, u32[]{:S(2)}, u32[]{:S(2)}) %all-to-all-start.5) | async-done | bytes 1048608 | tf_op jit(solution)/shard_map/all_to_all | solution.py:235
  469.7 2.1 collective-permute-done.11
  475.7 2.3 convolution_convert_fusion.2
  478.0 2.3 copy.83
  480.3 17.6 %collective-permute-done.12 = bf16[512,1024]{1,0:T(8,128)(2,1)S(1)} collective-permute-done((bf16[512,1024]{1,0:T(8,128)(2,1)S(1)}, bf16[512,1024]{1,0:T(8,128)(2,1)S(1)}, u32[]{:S(2)}, u32[]{:S(2)}) %collective-permute-start.12) | collective-permute-done | bytes 1048608 | tf_op jit(solution)/shard_map/ppermute | solution.py:246
  497.8 2.6 multiply_reduce_fusion.1
  500.7 3.2 add_convert_fusion.1
  504.0 4.0 maximum_select_fusion.1
  509.1 2.5 convert_element_type.203
  511.6 2.5 convert_element_type.204
  514.1 37.4 %psum.42 = f32[4,1024]{1,0:T(4,128)S(1)} all-reduce(f32[4,1024]{1,0:T(4,128)S(1)} %maximum_multiply_fusion), channel_id=1, replica_groups=mesh['dp'=8,'tensor'=4] {'dp','tensor'}, use_global_device_ids=true, to_apply=%region_13.14 | all-reduce | flops 4096 | bytes 32768 | tf_op jit(solution)/shard_map/psum | solution.py:357
  552.1 17.2 %all-reduce.9.cloned.1.call-done = (bf16[1024,4,128]{0,2,1:T(8,128)(2,1)}, bf16[1024,256]{1,0:T(8,128)(2,1)}) async-done(((bf16[1024,4,128]{0,2,1:T(8,128)(2,1)}, bf16[1024,256]{1,0:T(8,128)(2,1)}), (bf16[1024,4,128]{0,2,1:T(8,128)(2,1)}, bf16[1024,256]{1,0:T(8,128)(2,1)})) %all-reduce.9.cloned.1.call-update) | async-done | bytes 1572880 | tf_op jit(solution)/shard_map/psum | solution.py:354
  569.3 2.2 convert_element_type.201
  574.4 4.6 maximum_select_fusion.3
  (173 shorter events, 64.2 us)
Async XLA Ops:
  7.2 180.1 %copy-start = (bf16[1024,1024]{1,0:T(8,128)(2,1)S(1)}, bf16[1024,1024]{1,0:T(8,128)(2,1)}, u32[]{:S(2)}) copy-start(bf16[1024,1024]{1,0:T(8,128)(2,1)} %param.23) | copy-start | bytes 6291460
  10.3 3.7 copy-start.2
  11.0 2.9 copy-start.37
  11.0 4.2 copy-start.26
  16.8 20.8 %all-to-all-start = ((bf16[4,64,1024]{2,1,0:T(8,128)(2,1)}), bf16[4,64,1024]{2,1,0:T(8,128)(2,1)S(1)}, u32[]{:S(2)}, u32[]{:S(2)}) async-start(bf16[4,64,1024]{2,1,0:T(8,128)(2,1)} %bitcast.3), calls=%async_computation | async-start | bytes 1048576 | tf_op jit(solution)/shard_map/all_to_all | solution.py:235
  37.7 5.3 copy-start.18
  37.7 29.9 %all-to-all-start.1 = ((bf16[1024,4,128]{0,2,1:T(8,128)(2,1)}), bf16[1024,4,128]{0,2,1:T(8,128)(2,1)}, u32[]{:S(2)}, u32[]{:S(2)}) async-start(bf16[1024,4,128]{0,2,1:T(8,128)(2,1)} %bitcast.121), calls=%async_computation.1 | async-start | bytes 2097152 | tf_op jit(solution)/shard_map/all_to_all | solution.py:235
  72.1 28.3 %collective-permute-start = (bf16[4096,128]{0,1:T(8,128)(2,1)}, bf16[4096,128]{0,1:T(8,128)(2,1)S(1)}, u32[]{:S(2)}, u32[]{:S(2)}) collective-permute-start(bf16[4096,128]{0,1:T(8,128)(2,1)} %bitcast.96), channel_id=1, source_target_pairs={{0,4},{4,0},{8,12},{12,8},{16,20},{20,16},{24,28},{28,24},{1,5},{5... | collective-permute-start | bytes 3145736 | tf_op jit(solution)/shard_map/ppermute | solution.py:240
  133.1 17.9 %copy-start.19 = (bf16[256,1024]{1,0:T(8,128)(2,1)S(1)}, bf16[256,1024]{1,0:T(8,128)(2,1)}, u32[]{:S(2)}) copy-start(bf16[256,1024]{1,0:T(8,128)(2,1)} %param.20) | copy-start | bytes 1572868
  150.9 4.6 copy-start.21
  151.4 2.7 collective-permute-start.1
  155.5 25.5 %collective-permute-start.2 = (bf16[512,1024]{1,0:T(8,128)(2,1)}, bf16[512,1024]{1,0:T(8,128)(2,1)}, u32[]{:S(2)}, u32[]{:S(2)}) collective-permute-start(bf16[512,1024]{1,0:T(8,128)(2,1)} %add_convert_fusion.9), channel_id=1, source_target_pairs={{0,2},{1,3},{2,0},{3,1},{4,6},{5,7},{6,4},{7,5},{8,10},{9,11},{10,... | collective-permute-start | bytes 3145736 | tf_op jit(solution)/shard_map/ppermute | solution.py:246
  184.6 2.7 copy-start.31
  184.6 2.7 collective-permute-start.3
  186.6 61.8 %copy-start.9 = (bf16[1024,1024]{1,0:T(8,128)(2,1)}, bf16[1024,1024]{1,0:T(8,128)(2,1)S(1)}, u32[]{:S(2)}) copy-start(bf16[1024,1024]{1,0:T(8,128)(2,1)S(1)} %maximum_select_fusion.2) | copy-start | bytes 6291460
  186.7 3.7 copy-start.40
  187.3 3.0 copy-start.41
  190.4 11.9 %copy-start.45 = (bf16[1024,1024]{1,0:T(8,128)(2,1)}, bf16[1024,1024]{1,0:T(8,128)(2,1)S(1)}, u32[]{:S(2)}) copy-start(bf16[1024,1024]{1,0:T(8,128)(2,1)S(1)} %get-tuple-element.102) | copy-start | bytes 6291460
  195.4 4.0 copy-start.43
  196.7 2.7 collective-permute-start.7
  198.2 4.1 collective-permute-start.4
  200.7 26.1 %collective-permute-start.8 = (bf16[512,1024]{1,0:T(8,128)(2,1)S(1)}, bf16[512,1024]{1,0:T(8,128)(2,1)S(1)}, u32[]{:S(2)}, u32[]{:S(2)}) collective-permute-start(bf16[512,1024]{1,0:T(8,128)(2,1)S(1)} %add_convert_fusion.5), channel_id=1, source_target_pairs={{0,2},{1,3},{2,0},{3,1},{4,6},{5,7},{6,4},{7,5},{8,10},{9,11},{10,... | collective-permute-start | bytes 3145736 | tf_op jit(solution)/shard_map/ppermute | solution.py:246
  203.6 44.9 %collective-permute-start.5 = (bf16[512,1024]{1,0:T(8,128)(2,1)S(1)}, bf16[512,1024]{1,0:T(8,128)(2,1)S(1)}, u32[]{:S(2)}, u32[]{:S(2)}) collective-permute-start(bf16[512,1024]{1,0:T(8,128)(2,1)S(1)} %add_convert_fusion.7), channel_id=1, source_target_pairs={{0,2},{1,3},{2,0},{3,1},{4,6},{5,7},{6,4},{7,5},{8,10},{9,11},{10,... | collective-permute-start | bytes 3145736 | tf_op jit(solution)/shard_map/ppermute | solution.py:246
  251.4 3.4 collective-permute-start.9
  254.8 7.0 %copy-start.10 = (bf16[1024,1024]{1,0:T(8,128)(2,1)S(1)}, bf16[1024,1024]{1,0:T(8,128)(2,1)}, u32[]{:S(2)}) copy-start(bf16[1024,1024]{1,0:T(8,128)(2,1)} %copy-done.9) | copy-start | bytes 6291460
  258.0 18.6 %all-to-all-start.3 = ((bf16[4,64,1024]{2,1,0:T(8,128)(2,1)}), bf16[4,64,1024]{2,1,0:T(8,128)(2,1)S(1)}, u32[]{:S(2)}, u32[]{:S(2)}) async-start(bf16[4,64,1024]{2,1,0:T(8,128)(2,1)} %bitcast.18), calls=%async_computation.3 | async-start | bytes 1048576 | tf_op jit(solution)/shard_map/all_to_all | solution.py:235
  261.5 216.5 %all-reduce.11.cloned.1.call-start = ((), (), s32[]{:S(2)}) async-start(), calls=%async_computation.7 | async-start | bytes 9437184 | tf_op jit(solution)/shard_map/psum | solution.py:319
  261.8 5.5 copy-start.32
  261.8 5.5 copy-start.42
  261.8 5.5 copy-start.44
  267.3 3.9 copy-start.22
  332.9 55.4 %collective-permute-start.10 = (bf16[4096,128]{1,0:T(8,128)(2,1)}, bf16[4096,128]{1,0:T(8,128)(2,1)S(1)}, u32[]{:S(2)}, u32[]{:S(2)}) collective-permute-start(bf16[4096,128]{1,0:T(8,128)(2,1)} %get-tuple-element.34), channel_id=1, source_target_pairs={{0,4},{4,0},{8,12},{12,8},{16,20},{20,16},{24,28},{28,24},{1,5},{5... | collective-permute-start | bytes 3145736 | tf_op jit(solution)/shard_map/ppermute | solution.py:240
  384.9 25.2 %all-to-all-start.4 = ((bf16[64,4,1024]{2,0,1:T(8,128)(2,1)}), bf16[64,4,1024]{2,0,1:T(8,128)(2,1)S(1)}, u32[]{:S(2)}, u32[]{:S(2)}) async-start(bf16[64,4,1024]{2,0,1:T(8,128)(2,1)} %bitcast.86), calls=%async_computation.4 | async-start | bytes 1048576 | tf_op jit(solution)/shard_map/all_to_all | solution.py:235
  389.9 23.9 %copy-start.27 = (bf16[1024,256]{1,0:T(8,128)(2,1)S(1)}, bf16[1024,256]{1,0:T(8,128)(2,1)}, u32[]{:S(2)}) copy-start(bf16[1024,256]{1,0:T(8,128)(2,1)} %param.17) | copy-start | bytes 1572868
  410.1 59.1 %copy-start.28 = (bf16[64,4,1024]{2,0,1:T(8,128)(2,1)}, bf16[64,4,1024]{2,0,1:T(8,128)(2,1)S(1)}, u32[]{:S(2)}) copy-start(bf16[64,4,1024]{2,0,1:T(8,128)(2,1)S(1)} %all-to-all-done.4) | copy-start | bytes 1572868
  410.1 56.3 %all-to-all-start.5 = ((bf16[4,1024,128]{1,2,0:T(8,128)(2,1)}), bf16[4,1024,128]{1,2,0:T(8,128)(2,1)S(1)}, u32[]{:S(2)}, u32[]{:S(2)}) async-start(bf16[4,1024,128]{1,2,0:T(8,128)(2,1)} %copy.79), calls=%async_computation.5 | async-start | bytes 2097152 | tf_op jit(solution)/shard_map/all_to_all | solution.py:235
  413.6 155.7 %all-reduce.9.cloned.1.call-start = ((), (), s32[]{:S(2)}) async-start(), calls=%async_computation.6 | async-start | bytes 3145728 | tf_op jit(solution)/shard_map/psum | solution.py:354
  413.8 52.6 %copy-start.5 = (bf16[1024,4,128]{0,2,1:T(8,128)(2,1)S(1)}, bf16[1024,4,128]{0,2,1:T(8,128)(2,1)}, u32[]{:S(2)}) copy-start(bf16[1024,4,128]{0,2,1:T(8,128)(2,1)} %copy-done.4) | copy-start | bytes 3145732
  469.1 2.7 collective-permute-start.11
  472.6 25.3 %collective-permute-start.12 = (bf16[512,1024]{1,0:T(8,128)(2,1)S(1)}, bf16[512,1024]{1,0:T(8,128)(2,1)S(1)}, u32[]{:S(2)}, u32[]{:S(2)}) collective-permute-start(bf16[512,1024]{1,0:T(8,128)(2,1)S(1)} %add_convert_fusion.2), channel_id=1, source_target_pairs={{0,2},{1,3},{2,0},{3,1},{4,6},{5,7},{6,4},{7,5},{8,10},{9,11},{10,... | collective-permute-start | bytes 3145736 | tf_op jit(solution)/shard_map/ppermute | solution.py:246
  474.1 29.9 %collective-permute-start.6 = (bf16[512,1024]{1,0:T(8,128)(2,1)S(1)}, bf16[512,1024]{1,0:T(8,128)(2,1)}, u32[]{:S(2)}, u32[]{:S(2)}) collective-permute-start(bf16[512,1024]{1,0:T(8,128)(2,1)S(1)} %copy-done.11), channel_id=1, source_target_pairs={{0,1},{1,0},{2,3},{3,2},{4,5},{5,4},{6,7},{7,6},{8,9},{9,8},{10,11... | collective-permute-start | bytes 3145736 | tf_op jit(solution)/shard_map/ppermute | solution.py:243
  478.0 19.9 %copy-start.35 = (f32[1024]{0:T(1024)S(1)}, f32[1024]{0:T(1024)}, u32[]{:S(2)}) copy-start(f32[1024]{0:T(1024)} %param.15) | copy-start | bytes 12292
  497.8 2.9 copy-start.3
  497.8 2.9 slice-start
  504.0 4.0 copy-start.33
  504.0 5.1 copy-start.17
  504.0 70.4 %collective-permute-start.13 = (bf16[512,1024]{1,0:T(8,128)(2,1)}, bf16[512,1024]{1,0:T(8,128)(2,1)}, u32[]{:S(2)}, u32[]{:S(2)}) collective-permute-start(bf16[512,1024]{1,0:T(8,128)(2,1)} %add_convert_fusion.1), channel_id=1, source_target_pairs={{0,1},{1,0},{2,3},{3,2},{4,5},{5,4},{6,7},{7,6},{8,9},{9,8},{10,11... | collective-permute-start | bytes 3145736 | tf_op jit(solution)/shard_map/ppermute | solution.py:243
  573.1 5.9 %copy-start.1 = (bf16[1024,1024]{1,0:T(8,128)(2,1)S(1)}, bf16[1024,1024]{1,0:T(8,128)(2,1)}, u32[]{:S(2)}) copy-start(bf16[1024,1024]{1,0:T(8,128)(2,1)} %param.23) | copy-start | bytes 6291460
  (20 other events, 33.9 us)
Sparse Core Ops, SparseCore 0:
  274.3 203.4 all-reduce.10
  482.0 87.2 all-reduce.8
